TPU v7x, 32 devices: a whole 2x2x4 slice. The times are simulated.
32 devices in a mesh: fsdp: 8 (over z, core), rows: 4 (over y, x).
Axes of the slice: x: 2, y: 2, z: 4, core: 2. Of those that a mesh axis runs over, the one named last changes fastest.
Arguments:
- query_rows: bfloat16 [8, 1024, 1536], P('fsdp', 'rows'), may hold values from -6 to 6
- key_rows: bfloat16 [8, 1024, 1536], P('fsdp', 'rows'), may hold values from -6 to 6
- value_rows: bfloat16 [8, 1024, 1536], P('fsdp', 'rows'), may hold values from -6 to 6
- grad_out: bfloat16 [8, 1024, 3072], P('fsdp', 'rows'), may hold values from -6 to 6
- w_out: bfloat16 [1536, 3072], P('fsdp'), may hold values from -0.15625 to 0.15625
Outputs:
- grad_query: bfloat16 [8, 1024, 1536], P('fsdp', 'rows')
- grad_key: bfloat16 [8, 1024, 1536], P('fsdp', 'rows')
- grad_value: bfloat16 [8, 1024, 1536], P('fsdp', 'rows')
- grad_w_out: float32 [1536, 3072], P('fsdp')
All inputs are finite; a program needn't handle non-finite values.
Results may differ from a plain program's by a relative error of at most 0.02.
Values may be sent and summed in bfloat16 or wider, within the bound.
No kernel may reach another device: no remote copies, remote signals or barrier semaphores. Data moves between devices by JAX's collectives and lax.ppermute only.
A program may use at most 192 MiB of HBM per device.

v0:
```python
import math
import jax
import jax.numpy as jnp
from jax import lax
from jax.sharding import PartitionSpec as P

HDIM = 128
HEADS = 12
HW = 1536


def split_heads(array, count, groups):
    per_group = HEADS // groups
    return jnp.moveaxis(array.reshape(count, groups, per_group, HDIM), 1, 0)


def join_heads(array, count):
    return jnp.moveaxis(array, 0, 1).reshape(count, HW)


def local(query_rows, key_rows, value_rows, grad_out, w_out):
    tokens = query_rows.shape[1]
    factor = 1.0 / math.sqrt(HDIM)
    grad_flat = grad_out[0]
    groups = HEADS // 4
    grad_attn = lax.dot_general(
        grad_flat,
        lax.all_gather(w_out, "fsdp", axis=0, tiled=True),
        (((1,), (1,)), ((), ())),
        preferred_element_type=jnp.float32,
    ).astype(jnp.bfloat16)
    all_keys, all_values = (
        lax.all_gather(key_rows, "rows", axis=1, tiled=True),
        lax.all_gather(value_rows, "rows", axis=1, tiled=True),
    )
    length = all_keys.shape[1]

    def attend(inputs):
        query_heads, key_heads, value_heads, grad_heads = inputs
        scores = (
            jnp.einsum("qhd,khd->hqk", query_heads, key_heads, preferred_element_type=jnp.float32)
            * factor
        )
        probs = jax.nn.softmax(scores, axis=-1)
        probs_low = probs.astype(jnp.bfloat16)
        attended = jnp.einsum(
            "hqk,khd->qhd", probs_low, value_heads, preferred_element_type=jnp.float32
        )
        value_part = jnp.einsum(
            "hqk,qhd->khd", probs_low, grad_heads, preferred_element_type=jnp.float32
        )
        grad_probs = jnp.einsum(
            "qhd,khd->hqk", grad_heads, value_heads, preferred_element_type=jnp.float32
        )
        centre = jnp.sum(probs * grad_probs, axis=-1, keepdims=True)
        grad_scores = (probs * (grad_probs - centre)).astype(jnp.bfloat16)
        grad_query = (
            jnp.einsum("hqk,khd->qhd", grad_scores, key_heads, preferred_element_type=jnp.float32)
            * factor
        )
        key_part = (
            jnp.einsum("hqk,qhd->khd", grad_scores, query_heads, preferred_element_type=jnp.float32)
            * factor
        )
        return (
            attended.astype(jnp.bfloat16),
            grad_query.astype(jnp.bfloat16),
            key_part,
            value_part,
        )

    attended, grad_query, key_part, value_part = lax.map(
        attend,
        (
            split_heads(query_rows[0], tokens, groups),
            split_heads(all_keys[0], length, groups),
            split_heads(all_values[0], length, groups),
            split_heads(grad_attn, tokens, groups),
        ),
    )
    attended = join_heads(attended, tokens)
    grad_query = join_heads(grad_query, tokens).reshape(1, tokens, HW)
    key_part = join_heads(key_part, length)
    value_part = join_heads(value_part, length)
    grad_key, grad_value = (
        lax.psum_scatter(
            key_part.reshape(1, length, HW).astype(jnp.bfloat16),
            "rows",
            scatter_dimension=1,
            tiled=True,
        ).astype(jnp.float32),
        lax.psum_scatter(
            value_part.reshape(1, length, HW).astype(jnp.bfloat16),
            "rows",
            scatter_dimension=1,
            tiled=True,
        ).astype(jnp.float32),
    )
    term = lax.dot_general(
        attended, grad_flat, (((0,), (0,)), ((), ())), preferred_element_type=jnp.float32
    )
    partial_grad = lax.psum_scatter(
        lax.optimization_barrier(term.astype(jnp.bfloat16))
        .astype(jnp.float32)
        .astype(jnp.bfloat16),
        "fsdp",
        scatter_dimension=0,
        tiled=True,
    )
    grad_w_out = lax.psum(partial_grad, "rows").astype(jnp.float32)
    return (grad_query, grad_key.astype(jnp.bfloat16), grad_value.astype(jnp.bfloat16), grad_w_out)


def solution(mesh):
    in_specs = (
        P("fsdp", "rows", None),
        P("fsdp", "rows", None),
        P("fsdp", "rows", None),
        P("fsdp", "rows", None),
        P("fsdp", None),
    )
    out_specs = (
        P("fsdp", "rows", None),
        P("fsdp", "rows", None),
        P("fsdp", "rows", None),
        P("fsdp", None),
    )
    return jax.shard_map(local, mesh=mesh, in_specs=in_specs, out_specs=out_specs, check_vma=False)
```

profile of v0, /device:TPU:0, one launch (start us, length us, event | category | flops | bytes accessed | tf_op | source)
XLA Modules:
  0.0 541.0 jit_solution(524409484215932579)
XLA Ops:
  8.7 2.3 copy.24
  11.4 45.0 %all-gather.4.cloned.1.call-done = bf16[1,1024,1536]{2,1,0:T(8,128)(2,1)} async-done(((bf16[1,256,1536]{2,1,0:T(8,128)(2,1)}), bf16[1,1024,1536]{2,1,0:T(8,128)(2,1)}) %all-gather.4.cloned.1.call-update) | async-done | bytes 3145744 | tf_op jit(solution)/shard_map/all_gather | solution.py:34
  56.4 4.7 copy.22
  61.2 87.7 %all-gather.8.cloned.1.call-done = bf16[1536,3072]{1,0:T(8,128)(2,1)} async-done(((bf16[192,3072]{1,0:T(8,128)(2,1)}), bf16[1536,3072]{1,0:T(8,128)(2,1)}) %all-gather.8.cloned.1.call-update) | async-done | bytes 9437200 | tf_op jit(solution)/shard_map/all_gather | solution.py:28
  148.8 7.2 %convolution_convert_fusion.2 = bf16[256,1536]{1,0:T(8,128)(2,1)} fusion(bf16[1536,3072]{1,0:T(8,128)(2,1)} %all-gather.8.cloned.1.call-done, bf16[1,256,3072]{2,1,0:T(8,128)(2,1)S(1)} %copy-done), kind=kOutput, calls=%fused_computation.45 | convolution fusion | flops 2416312320 | bytes 11796480 | tf_op jit(solution)/shard_map/dot_general | solution.py:26
  158.8 34.6 %all-gather.6.cloned.1.call-done = bf16[1,1024,1536]{1,2,0:T(8,128)(2,1)} async-done(((bf16[1,256,1536]{1,2,0:T(8,128)(2,1)}), bf16[1,1024,1536]{1,2,0:T(8,128)(2,1)}) %all-gather.6.cloned.1.call-update) | async-done | bytes 3145744 | tf_op jit(solution)/shard_map/all_gather | solution.py:33
  193.4 84.2 %while.16 = (s32[]{:T(128)}, bf16[3,256,4,128]{1,3,2,0:T(8,128)(2,1)}, bf16[3,256,4,128]{1,3,2,0:T(8,128)(2,1)}, bf16[3,1024,4,128]{1,3,2,0:T(8,128)(2,1)}, bf16...) while((s32[]{:T(128)}, ...), condition=%wide.region_4.5_spmd, body=%wide.region_0.4_spmd.sunk | while | flops 1633554432 | bytes 124291328 | solution.py:72
  195.4 3.2 fusion.81
  198.5 6.7 %fusion.82 = bf16[3,256,4,128]{1,3,2,0:T(8,128)(2,1)} fusion(bf16[3,256,4,128]{1,3,2,0:T(8,128)(2,1)} %get-tuple-element.163, s32[]{:T(128)S(6)} %copy.51, bf16[3,1024,4,128]{1,3,2,0:T(8,128)(2,1)} %get-tuple-element.177, f32[4,256]{1,0:T(4,128)S(1)} %get-tuple-element.148, f32[4,256,1024]{2,1,0:T(8,128)} %copy-done.2), kind=kOutput, calls=%fused_computation.14.clone.1 | convolution fusion | flops 273811456 | bytes 9704448 | tf_op jit(solution)/shard_map/while/body/eval_jaxpr/hqk,khd->qhd/dot_general | solution.py:46
  205.3 6.6 %bitcast_dynamic-update-slice_fusion.5 = bf16[3,1024,4,128]{1,3,2,0:T(8,128)(2,1)} fusion(bf16[3,1024,4,128]{1,3,2,0:T(8,128)(2,1)} %get-tuple-element.166, s32[]{:T(128)S(6)} %copy.51, bf16[3,256,4,128]{3,1,2,0:T(8,128)(2,1)S(1)} %copy-done.6, f32[4,256]{1,0:T(4,128)S(1)} %get-tuple-element.148, f32[4,256,1024]{2,1,0:T(8,128)} %copy-done.2), kind=kOutput, calls=%fused_computation.6.clone.1 | convolution fusion | flops 273680384 | bytes 10753024 | tf_op jit(solution)/shard_map/while/body/eval_jaxpr/hqk,qhd->khd/dot_general | solution.py:49
  211.9 3.4 multiply_reduce_fusion.3
  216.3 3.0 fusion.83
  221.5 2.0 fusion.80
  223.5 3.2 fusion.81
  226.6 6.7 %fusion.82 = bf16[3,256,4,128]{1,3,2,0:T(8,128)(2,1)} fusion(bf16[3,256,4,128]{1,3,2,0:T(8,128)(2,1)} %get-tuple-element.163, s32[]{:T(128)S(6)} %copy.51, bf16[3,1024,4,128]{1,3,2,0:T(8,128)(2,1)} %get-tuple-element.177, f32[4,256]{1,0:T(4,128)S(1)} %get-tuple-element.148, f32[4,256,1024]{2,1,0:T(8,128)} %copy-done.2), kind=kOutput, calls=%fused_computation.14.clone.1 | convolution fusion | flops 273811456 | bytes 9704448 | tf_op jit(solution)/shard_map/while/body/eval_jaxpr/hqk,khd->qhd/dot_general | solution.py:46
  233.4 6.6 %bitcast_dynamic-update-slice_fusion.5 = bf16[3,1024,4,128]{1,3,2,0:T(8,128)(2,1)} fusion(bf16[3,1024,4,128]{1,3,2,0:T(8,128)(2,1)} %get-tuple-element.166, s32[]{:T(128)S(6)} %copy.51, bf16[3,256,4,128]{3,1,2,0:T(8,128)(2,1)S(1)} %copy-done.6, f32[4,256]{1,0:T(4,128)S(1)} %get-tuple-element.148, f32[4,256,1024]{2,1,0:T(8,128)} %copy-done.2), kind=kOutput, calls=%fused_computation.6.clone.1 | convolution fusion | flops 273680384 | bytes 10753024 | tf_op jit(solution)/shard_map/while/body/eval_jaxpr/hqk,qhd->khd/dot_general | solution.py:49
  240.0 3.4 multiply_reduce_fusion.3
  244.4 3.0 fusion.83
  249.5 2.0 fusion.80
  251.5 3.2 fusion.81
  254.7 6.7 %fusion.82 = bf16[3,256,4,128]{1,3,2,0:T(8,128)(2,1)} fusion(bf16[3,256,4,128]{1,3,2,0:T(8,128)(2,1)} %get-tuple-element.163, s32[]{:T(128)S(6)} %copy.51, bf16[3,1024,4,128]{1,3,2,0:T(8,128)(2,1)} %get-tuple-element.177, f32[4,256]{1,0:T(4,128)S(1)} %get-tuple-element.148, f32[4,256,1024]{2,1,0:T(8,128)} %copy-done.2), kind=kOutput, calls=%fused_computation.14.clone.1 | convolution fusion | flops 273811456 | bytes 9704448 | tf_op jit(solution)/shard_map/while/body/eval_jaxpr/hqk,khd->qhd/dot_general | solution.py:46
  261.5 6.6 %bitcast_dynamic-update-slice_fusion.5 = bf16[3,1024,4,128]{1,3,2,0:T(8,128)(2,1)} fusion(bf16[3,1024,4,128]{1,3,2,0:T(8,128)(2,1)} %get-tuple-element.166, s32[]{:T(128)S(6)} %copy.51, bf16[3,256,4,128]{3,1,2,0:T(8,128)(2,1)S(1)} %copy-done.6, f32[4,256]{1,0:T(4,128)S(1)} %get-tuple-element.148, f32[4,256,1024]{2,1,0:T(8,128)} %copy-done.2), kind=kOutput, calls=%fused_computation.6.clone.1 | convolution fusion | flops 273680384 | bytes 10753024 | tf_op jit(solution)/shard_map/while/body/eval_jaxpr/hqk,qhd->khd/dot_general | solution.py:49
  268.0 3.4 multiply_reduce_fusion.3
  272.4 3.0 fusion.83
  277.6 6.2 %convolution_convert_fusion.1 = bf16[1536,3072]{1,0:T(8,128)(2,1)} fusion(bf16[256,1536]{0,1:T(8,128)(2,1)} %bitcast.114, bf16[1,256,3072]{2,1,0:T(8,128)(2,1)S(1)} %copy-done), kind=kOutput, calls=%fused_computation.44 | convolution fusion | flops 2420637696 | bytes 11796480 | tf_op jit(solution)/shard_map/dot_general | solution.py:99
  283.9 99.5 %reduce-scatter.8.cloned.1.call-done = bf16[192,3072]{1,0:T(8,128)(2,1)} async-done(((bf16[1536,3072]{1,0:T(8,128)(2,1)}), bf16[192,3072]{1,0:T(8,128)(2,1)}) %reduce-scatter.8.cloned.1.call-update) | async-done | bytes 1179664 | tf_op jit(solution)/shard_map/reduce_scatter | solution.py:102
  383.6 4.7 copy.37
  388.3 4.7 copy.36
  394.2 45.1 %all-reduce.2.cloned.1.call-done = bf16[192,3072]{1,0:T(8,128)(2,1)} async-done(((bf16[192,3072]{1,0:T(8,128)(2,1)}), bf16[192,3072]{1,0:T(8,128)(2,1)}) %all-reduce.2.cloned.1.call-update) | async-done | bytes 1179664 | tf_op jit(solution)/shard_map/psum | solution.py:110
  439.3 2.9 convert_element_type.75
  442.2 44.4 %reduce-scatter.6.cloned.1.call-done = bf16[1,256,1536]{2,1,0:T(8,128)(2,1)} async-done(((bf16[1,1024,1536]{2,1,0:T(8,128)(2,1)}), bf16[1,256,1536]{2,1,0:T(8,128)(2,1)}) %reduce-scatter.6.cloned.1.call-update) | async-done | bytes 786448 | tf_op jit(solution)/shard_map/reduce_scatter | solution.py:92
  486.6 47.5 %reduce-scatter.4.cloned.1.call-done = bf16[1,256,1536]{2,1,0:T(8,128)(2,1)} async-done(((bf16[1,1024,1536]{2,1,0:T(8,128)(2,1)}), bf16[1,256,1536]{2,1,0:T(8,128)(2,1)}) %reduce-scatter.4.cloned.1.call-update) | async-done | bytes 786448 | tf_op jit(solution)/shard_map/reduce_scatter | solution.py:86
  (65 shorter events, 17.2 us)
Async XLA Ops:
  7.2 141.7 %copy-start = (bf16[1,256,3072]{2,1,0:T(8,128)(2,1)S(1)}, bf16[1,256,3072]{2,1,0:T(8,128)(2,1)}, u32[]{:S(2)}) copy-start(bf16[1,256,3072]{2,1,0:T(8,128)(2,1)} %param.10) | copy-start | bytes 4718596
  7.2 3.9 copy-start.5
  7.2 49.3 %all-gather.4.cloned.1.call-start = ((), (), s32[]{:S(2)}) async-start(), calls=%async_computation.3 | async-start | bytes 3932160 | tf_op jit(solution)/shard_map/all_gather | solution.py:34
  7.9 140.9 %all-gather.8.cloned.1.call-start = ((), (), s32[]{:S(2)}) async-start(), calls=%async_computation.5 | async-start | bytes 10616832 | tf_op jit(solution)/shard_map/all_gather | solution.py:28
  8.7 184.7 %all-gather.6.cloned.1.call-start = ((), (), s32[]{:S(2)}) async-start(), calls=%async_computation.4 | async-start | bytes 3932160 | tf_op jit(solution)/shard_map/all_gather | solution.py:33
  11.0 372.5 %reduce-scatter.8.cloned.1.call-start = ((), (), s32[]{:S(2)}) async-start(), calls=%async_computation.8 | async-start | bytes 10616832 | tf_op jit(solution)/shard_map/reduce_scatter | solution.py:102
  195.4 3.2 copy-start.2
  198.5 6.7 %copy-start.6 = (bf16[3,256,4,128]{3,1,2,0:T(8,128)(2,1)S(1)}, bf16[3,256,4,128]{3,1,2,0:T(8,128)(2,1)}, u32[]{:S(2)}) copy-start(bf16[3,256,4,128]{3,1,2,0:T(8,128)(2,1)} %get-tuple-element.180) | copy-start | bytes 2359300 | tf_op jit(solution)/shard_map/while
  211.9 3.7 copy-start.1
  215.6 3.7 copy-start.3
  219.8 1.7 copy-start.4
  223.4 3.2 copy-start.2
  226.6 6.7 %copy-start.6 = (bf16[3,256,4,128]{3,1,2,0:T(8,128)(2,1)S(1)}, bf16[3,256,4,128]{3,1,2,0:T(8,128)(2,1)}, u32[]{:S(2)}) copy-start(bf16[3,256,4,128]{3,1,2,0:T(8,128)(2,1)} %get-tuple-element.180) | copy-start | bytes 2359300 | tf_op jit(solution)/shard_map/while
  240.0 3.7 copy-start.1
  243.7 3.7 copy-start.3
  247.9 1.7 copy-start.4
  251.5 3.2 copy-start.2
  254.7 6.7 %copy-start.6 = (bf16[3,256,4,128]{3,1,2,0:T(8,128)(2,1)S(1)}, bf16[3,256,4,128]{3,1,2,0:T(8,128)(2,1)}, u32[]{:S(2)}) copy-start(bf16[3,256,4,128]{3,1,2,0:T(8,128)(2,1)} %get-tuple-element.180) | copy-start | bytes 2359300 | tf_op jit(solution)/shard_map/while
  268.0 3.7 copy-start.1
  271.8 3.7 copy-start.3
  276.0 1.7 copy-start.4
  283.9 155.4 %all-reduce.2.cloned.1.call-start = ((), (), s32[]{:S(2)}) async-start(), calls=%async_computation.9 | async-start | bytes 2359296 | tf_op jit(solution)/shard_map/psum | solution.py:110
  383.5 103.1 %reduce-scatter.6.cloned.1.call-start = ((), (), s32[]{:S(2)}) async-start(), calls=%async_computation.7 | async-start | bytes 3932160 | tf_op jit(solution)/shard_map/reduce_scatter | solution.py:92
  388.2 145.9 %reduce-scatter.4.cloned.1.call-start = ((), (), s32[]{:S(2)}) async-start(), calls=%async_computation.6 | async-start | bytes 3932160 | tf_op jit(solution)/shard_map/reduce_scatter | solution.py:86
  388.3 4.7 copy-start.7
Sparse Core Ops, SparseCore 0:
  9.8 46.5 all-gather.3
  58.1 90.6 all-gather.7
  151.2 42.1 all-gather.5
  284.0 99.4 reduce-scatter.7
  386.4 52.8 all-reduce.1
  442.7 43.8 reduce-scatter.5
  490.2 43.8 reduce-scatter.3
where the time goes:
time: 542 us; the launch traced here: 541 us
  waiting for transfers between devices  405 us (75%)
  matrix products  80.2 us (15%)
  local copies, waits for them, and re-layouts  26.5 us (5%)
  other arithmetic  14.4 us (3%)
  between operations  14.2 us (3%)
    reduce_scatter x1, waiting for transfers between devices, local(): lax.psum_scatter(lax.optimization_barrier(term.astype(jnp.bfloat16)).asty...  99.5 us
    all_gather x1, waiting for transfers between devices, local(): lax.all_gather(w_out, 'fsdp', axis=0, tiled=True)  87.7 us
    reduce_scatter x1, waiting for transfers between devices, local(): lax.psum_scatter(key_part.reshape(1, length, HW).astype(jnp.bfloat16), 'r...  47.5 us
    psum x1, waiting for transfers between devices, local(): grad_w_out = lax.psum(partial_grad, 'rows').astype(jnp.float32)  45.1 us
    all_gather x1, waiting for transfers between devices, local(): lax.all_gather(value_rows, 'rows', axis=1, tiled=True)  45 us
    reduce_scatter x1, waiting for transfers between devices, local(): lax.psum_scatter(value_part.reshape(1, length, HW).astype(jnp.bfloat16),...  44.4 us
    all_gather x1, waiting for transfers between devices, local(): lax.all_gather(key_rows, 'rows', axis=1, tiled=True)  34.6 us
    dot_general x3, matrix products, attend(): jnp.einsum('hqk,khd->qhd', probs_low, value_heads, preferred_element_type...  20.2 us
  transfers between devices with their start and end apart: 7, of which 7 were waited for; matrix products, arithmetic and copies ran while one was open for 6% of the time, Pallas kernels for 0%

commit v1 on v0

--- a/solution.py
+++ b/solution.py
@@ -107,7 +107,7 @@
         scatter_dimension=0,
         tiled=True,
     )
-    grad_w_out = lax.psum(partial_grad, "rows").astype(jnp.float32)
+    grad_w_out = jnp.sum(lax.all_gather(partial_grad, "rows"), axis=0).astype(jnp.float32)
     return (grad_query, grad_key.astype(jnp.bfloat16), grad_value.astype(jnp.bfloat16), grad_w_out)
 
 

time: 542 us -> 543 us (level)
    all_gather x0 -> x1, waiting for transfers between devices: none -> 46.2 us  [local(): lax.all_gather(partial_grad, 'rows')]
    psum x1 -> x0, waiting for transfers between devices: 45.1 us -> none  [local(): grad_w_out = lax.psum(partial_grad, 'rows').astype(jnp.float32)]
where the time goes in v1:
time: 543 us; the launch traced here: 542 us
  waiting for transfers between devices  404 us (74%)
  matrix products  80.2 us (15%)
  local copies, waits for them, and re-layouts  26.7 us (5%)
  other arithmetic  16.5 us (3%)
  between operations  14.2 us (3%)
    reduce_scatter x1, waiting for transfers between devices, local(): lax.psum_scatter(lax.optimization_barrier(term.astype(jnp.bfloat16)).asty...  99.5 us
    all_gather x1, waiting for transfers between devices, local(): lax.all_gather(w_out, 'fsdp', axis=0, tiled=True)  87.7 us
    reduce_scatter x1, waiting for transfers between devices, local(): lax.psum_scatter(key_part.reshape(1, length, HW).astype(jnp.bfloat16), 'r...  47.5 us
    all_gather x1, waiting for transfers between devices, local(): lax.all_gather(partial_grad, 'rows')  46.2 us
    all_gather x1, waiting for transfers between devices, local(): lax.all_gather(value_rows, 'rows', axis=1, tiled=True)  45 us
    reduce_scatter x1, waiting for transfers between devices, local(): lax.psum_scatter(value_part.reshape(1, length, HW).astype(jnp.bfloat16),...  42.4 us
    all_gather x1, waiting for transfers between devices, local(): lax.all_gather(key_rows, 'rows', axis=1, tiled=True)  34.6 us
    dot_general x3, matrix products, attend(): jnp.einsum('hqk,khd->qhd', probs_low, value_heads, preferred_element_type...  20.2 us
  transfers between devices with their start and end apart: 7, of which 7 were waited for; matrix products, arithmetic and copies ran while one was open for 6% of the time, Pallas kernels for 0%

profile of v1, /device:TPU:0, one launch (start us, length us, event | category | flops | bytes accessed | tf_op | source)
XLA Modules:
  0.0 542.3 jit_solution(1449971151170399442)
XLA Ops:
  8.7 2.3 copy.24
  11.4 45.0 %all-gather.6.cloned.1.call-done = bf16[1,1024,1536]{2,1,0:T(8,128)(2,1)} async-done(((bf16[1,256,1536]{2,1,0:T(8,128)(2,1)}), bf16[1,1024,1536]{2,1,0:T(8,128)(2,1)}) %all-gather.6.cloned.1.call-update) | async-done | bytes 3145744 | tf_op jit(solution)/shard_map/all_gather | solution.py:34
  56.4 4.7 copy.22
  61.2 87.7 %all-gather.10.cloned.1.call-done = bf16[1536,3072]{1,0:T(8,128)(2,1)} async-done(((bf16[192,3072]{1,0:T(8,128)(2,1)}), bf16[1536,3072]{1,0:T(8,128)(2,1)}) %all-gather.10.cloned.1.call-update) | async-done | bytes 9437200 | tf_op jit(solution)/shard_map/all_gather | solution.py:28
  148.8 7.2 %convolution_convert_fusion.2 = bf16[256,1536]{1,0:T(8,128)(2,1)} fusion(bf16[1536,3072]{1,0:T(8,128)(2,1)} %all-gather.10.cloned.1.call-done, bf16[1,256,3072]{2,1,0:T(8,128)(2,1)S(1)} %copy-done), kind=kOutput, calls=%fused_computation.45 | convolution fusion | flops 2416312320 | bytes 11796480 | tf_op jit(solution)/shard_map/dot_general | solution.py:26
  158.8 34.6 %all-gather.8.cloned.1.call-done = bf16[1,1024,1536]{1,2,0:T(8,128)(2,1)} async-done(((bf16[1,256,1536]{1,2,0:T(8,128)(2,1)}), bf16[1,1024,1536]{1,2,0:T(8,128)(2,1)}) %all-gather.8.cloned.1.call-update) | async-done | bytes 3145744 | tf_op jit(solution)/shard_map/all_gather | solution.py:33
  193.4 84.2 %while.16 = (s32[]{:T(128)}, bf16[3,256,4,128]{1,3,2,0:T(8,128)(2,1)}, bf16[3,256,4,128]{1,3,2,0:T(8,128)(2,1)}, bf16[3,1024,4,128]{1,3,2,0:T(8,128)(2,1)}, bf16...) while((s32[]{:T(128)}, ...), condition=%wide.region_4.5_spmd, body=%wide.region_0.4_spmd.sunk | while | flops 1633554432 | bytes 124291328 | solution.py:72
  195.4 3.2 fusion.81
  198.5 6.7 %fusion.82 = bf16[3,256,4,128]{1,3,2,0:T(8,128)(2,1)} fusion(bf16[3,256,4,128]{1,3,2,0:T(8,128)(2,1)} %get-tuple-element.163, s32[]{:T(128)S(6)} %copy.51, bf16[3,1024,4,128]{1,3,2,0:T(8,128)(2,1)} %get-tuple-element.177, f32[4,256]{1,0:T(4,128)S(1)} %get-tuple-element.148, f32[4,256,1024]{2,1,0:T(8,128)} %copy-done.2), kind=kOutput, calls=%fused_computation.14.clone.1 | convolution fusion | flops 273811456 | bytes 9704448 | tf_op jit(solution)/shard_map/while/body/eval_jaxpr/hqk,khd->qhd/dot_general | solution.py:46
  205.3 6.6 %bitcast_dynamic-update-slice_fusion.5 = bf16[3,1024,4,128]{1,3,2,0:T(8,128)(2,1)} fusion(bf16[3,1024,4,128]{1,3,2,0:T(8,128)(2,1)} %get-tuple-element.166, s32[]{:T(128)S(6)} %copy.51, bf16[3,256,4,128]{3,1,2,0:T(8,128)(2,1)S(1)} %copy-done.6, f32[4,256]{1,0:T(4,128)S(1)} %get-tuple-element.148, f32[4,256,1024]{2,1,0:T(8,128)} %copy-done.2), kind=kOutput, calls=%fused_computation.6.clone.1 | convolution fusion | flops 273680384 | bytes 10753024 | tf_op jit(solution)/shard_map/while/body/eval_jaxpr/hqk,qhd->khd/dot_general | solution.py:49
  211.9 3.4 multiply_reduce_fusion.3
  216.3 3.0 fusion.83
  221.5 2.0 fusion.80
  223.5 3.2 fusion.81
  226.6 6.7 %fusion.82 = bf16[3,256,4,128]{1,3,2,0:T(8,128)(2,1)} fusion(bf16[3,256,4,128]{1,3,2,0:T(8,128)(2,1)} %get-tuple-element.163, s32[]{:T(128)S(6)} %copy.51, bf16[3,1024,4,128]{1,3,2,0:T(8,128)(2,1)} %get-tuple-element.177, f32[4,256]{1,0:T(4,128)S(1)} %get-tuple-element.148, f32[4,256,1024]{2,1,0:T(8,128)} %copy-done.2), kind=kOutput, calls=%fused_computation.14.clone.1 | convolution fusion | flops 273811456 | bytes 9704448 | tf_op jit(solution)/shard_map/while/body/eval_jaxpr/hqk,khd->qhd/dot_general | solution.py:46
  233.4 6.6 %bitcast_dynamic-update-slice_fusion.5 = bf16[3,1024,4,128]{1,3,2,0:T(8,128)(2,1)} fusion(bf16[3,1024,4,128]{1,3,2,0:T(8,128)(2,1)} %get-tuple-element.166, s32[]{:T(128)S(6)} %copy.51, bf16[3,256,4,128]{3,1,2,0:T(8,128)(2,1)S(1)} %copy-done.6, f32[4,256]{1,0:T(4,128)S(1)} %get-tuple-element.148, f32[4,256,1024]{2,1,0:T(8,128)} %copy-done.2), kind=kOutput, calls=%fused_computation.6.clone.1 | convolution fusion | flops 273680384 | bytes 10753024 | tf_op jit(solution)/shard_map/while/body/eval_jaxpr/hqk,qhd->khd/dot_general | solution.py:49
  240.0 3.4 multiply_reduce_fusion.3
  244.4 3.0 fusion.83
  249.5 2.0 fusion.80
  251.5 3.2 fusion.81
  254.7 6.7 %fusion.82 = bf16[3,256,4,128]{1,3,2,0:T(8,128)(2,1)} fusion(bf16[3,256,4,128]{1,3,2,0:T(8,128)(2,1)} %get-tuple-element.163, s32[]{:T(128)S(6)} %copy.51, bf16[3,1024,4,128]{1,3,2,0:T(8,128)(2,1)} %get-tuple-element.177, f32[4,256]{1,0:T(4,128)S(1)} %get-tuple-element.148, f32[4,256,1024]{2,1,0:T(8,128)} %copy-done.2), kind=kOutput, calls=%fused_computation.14.clone.1 | convolution fusion | flops 273811456 | bytes 9704448 | tf_op jit(solution)/shard_map/while/body/eval_jaxpr/hqk,khd->qhd/dot_general | solution.py:46
  261.5 6.6 %bitcast_dynamic-update-slice_fusion.5 = bf16[3,1024,4,128]{1,3,2,0:T(8,128)(2,1)} fusion(bf16[3,1024,4,128]{1,3,2,0:T(8,128)(2,1)} %get-tuple-element.166, s32[]{:T(128)S(6)} %copy.51, bf16[3,256,4,128]{3,1,2,0:T(8,128)(2,1)S(1)} %copy-done.6, f32[4,256]{1,0:T(4,128)S(1)} %get-tuple-element.148, f32[4,256,1024]{2,1,0:T(8,128)} %copy-done.2), kind=kOutput, calls=%fused_computation.6.clone.1 | convolution fusion | flops 273680384 | bytes 10753024 | tf_op jit(solution)/shard_map/while/body/eval_jaxpr/hqk,qhd->khd/dot_general | solution.py:49
  268.0 3.4 multiply_reduce_fusion.3
  272.4 3.0 fusion.83
  277.6 6.2 %convolution_convert_fusion.1 = bf16[1536,3072]{1,0:T(8,128)(2,1)} fusion(bf16[256,1536]{0,1:T(8,128)(2,1)} %bitcast.116, bf16[1,256,3072]{2,1,0:T(8,128)(2,1)S(1)} %copy-done), kind=kOutput, calls=%fused_computation.44 | convolution fusion | flops 2420637696 | bytes 11796480 | tf_op jit(solution)/shard_map/dot_general | solution.py:99
  283.9 99.5 %reduce-scatter.8.cloned.1.call-done = bf16[192,3072]{1,0:T(8,128)(2,1)} async-done(((bf16[1536,3072]{1,0:T(8,128)(2,1)}), bf16[192,3072]{1,0:T(8,128)(2,1)}) %reduce-scatter.8.cloned.1.call-update) | async-done | bytes 1179664 | tf_op jit(solution)/shard_map/reduce_scatter | solution.py:102
  383.6 4.6 copy.37
  388.3 5.0 copy.36
  394.4 46.2 %all-gather.12.cloned.1.call-done = bf16[768,3072]{1,0:T(8,128)(2,1)} async-done(((bf16[192,3072]{1,0:T(8,128)(2,1)}), bf16[768,3072]{1,0:T(8,128)(2,1)}) %all-gather.12.cloned.1.call-update) | async-done | bytes 4718608 | tf_op jit(solution)/shard_map/all_gather | solution.py:110
  440.6 3.3 reduce_sum.30
  445.6 42.4 %reduce-scatter.6.cloned.1.call-done = bf16[1,256,1536]{2,1,0:T(8,128)(2,1)} async-done(((bf16[1,1024,1536]{2,1,0:T(8,128)(2,1)}), bf16[1,256,1536]{2,1,0:T(8,128)(2,1)}) %reduce-scatter.6.cloned.1.call-update) | async-done | bytes 786448 | tf_op jit(solution)/shard_map/reduce_scatter | solution.py:92
  488.0 47.5 %reduce-scatter.4.cloned.1.call-done = bf16[1,256,1536]{2,1,0:T(8,128)(2,1)} async-done(((bf16[1,1024,1536]{2,1,0:T(8,128)(2,1)}), bf16[1,256,1536]{2,1,0:T(8,128)(2,1)}) %reduce-scatter.4.cloned.1.call-update) | async-done | bytes 786448 | tf_op jit(solution)/shard_map/reduce_scatter | solution.py:86
  (66 shorter events, 18.9 us)
Async XLA Ops:
  7.2 141.7 %copy-start = (bf16[1,256,3072]{2,1,0:T(8,128)(2,1)S(1)}, bf16[1,256,3072]{2,1,0:T(8,128)(2,1)}, u32[]{:S(2)}) copy-start(bf16[1,256,3072]{2,1,0:T(8,128)(2,1)} %param.10) | copy-start | bytes 4718596
  7.2 3.9 copy-start.5
  7.2 49.3 %all-gather.6.cloned.1.call-start = ((), (), s32[]{:S(2)}) async-start(), calls=%async_computation.3 | async-start | bytes 3932160 | tf_op jit(solution)/shard_map/all_gather | solution.py:34
  7.9 140.9 %all-gather.10.cloned.1.call-start = ((), (), s32[]{:S(2)}) async-start(), calls=%async_computation.5 | async-start | bytes 10616832 | tf_op jit(solution)/shard_map/all_gather | solution.py:28
  8.7 184.7 %all-gather.8.cloned.1.call-start = ((), (), s32[]{:S(2)}) async-start(), calls=%async_computation.4 | async-start | bytes 3932160 | tf_op jit(solution)/shard_map/all_gather | solution.py:33
  11.0 372.5 %reduce-scatter.8.cloned.1.call-start = ((), (), s32[]{:S(2)}) async-start(), calls=%async_computation.8 | async-start | bytes 10616832 | tf_op jit(solution)/shard_map/reduce_scatter | solution.py:102
  195.4 3.2 copy-start.2
  198.5 6.7 %copy-start.6 = (bf16[3,256,4,128]{3,1,2,0:T(8,128)(2,1)S(1)}, bf16[3,256,4,128]{3,1,2,0:T(8,128)(2,1)}, u32[]{:S(2)}) copy-start(bf16[3,256,4,128]{3,1,2,0:T(8,128)(2,1)} %get-tuple-element.180) | copy-start | bytes 2359300 | tf_op jit(solution)/shard_map/while
  211.9 3.7 copy-start.1
  215.6 3.7 copy-start.3
  219.8 1.7 copy-start.4
  223.4 3.2 copy-start.2
  226.6 6.7 %copy-start.6 = (bf16[3,256,4,128]{3,1,2,0:T(8,128)(2,1)S(1)}, bf16[3,256,4,128]{3,1,2,0:T(8,128)(2,1)}, u32[]{:S(2)}) copy-start(bf16[3,256,4,128]{3,1,2,0:T(8,128)(2,1)} %get-tuple-element.180) | copy-start | bytes 2359300 | tf_op jit(solution)/shard_map/while
  240.0 3.7 copy-start.1
  243.7 3.7 copy-start.3
  247.9 1.7 copy-start.4
  251.5 3.2 copy-start.2
  254.7 6.7 %copy-start.6 = (bf16[3,256,4,128]{3,1,2,0:T(8,128)(2,1)S(1)}, bf16[3,256,4,128]{3,1,2,0:T(8,128)(2,1)}, u32[]{:S(2)}) copy-start(bf16[3,256,4,128]{3,1,2,0:T(8,128)(2,1)} %get-tuple-element.180) | copy-start | bytes 2359300 | tf_op jit(solution)/shard_map/while
  268.0 3.7 copy-start.1
  271.8 3.7 copy-start.3
  276.0 1.7 copy-start.4
  283.9 156.7 %all-gather.12.cloned.1.call-start = ((), (), s32[]{:S(2)}) async-start(), calls=%async_computation.9 | async-start | bytes 5898240 | tf_op jit(solution)/shard_map/all_gather | solution.py:110
  383.5 104.4 %reduce-scatter.6.cloned.1.call-start = ((), (), s32[]{:S(2)}) async-start(), calls=%async_computation.7 | async-start | bytes 3932160 | tf_op jit(solution)/shard_map/reduce_scatter | solution.py:92
  388.2 147.2 %reduce-scatter.4.cloned.1.call-start = ((), (), s32[]{:S(2)}) async-start(), calls=%async_computation.6 | async-start | bytes 3932160 | tf_op jit(solution)/shard_map/reduce_scatter | solution.py:86
  388.3 5.0 copy-start.7
Sparse Core Ops, SparseCore 0:
  9.8 46.5 all-gather.5
  58.1 90.6 all-gather.9
  151.2 42.1 all-gather.7
  284.0 99.4 reduce-scatter.7
  385.2 55.3 all-gather.11
  444.0 43.8 reduce-scatter.5
  491.5 43.8 reduce-scatter.3
